TPU v7x, 32 devices: a whole 2x2x4 slice. The times are simulated.
32 devices in a mesh: grp: 2 (over y), tm: 4 (over z), space: 4 (over x, core).
Axes of the slice: x: 2, y: 2, z: 4, core: 2. Of those that a mesh axis runs over, the one named last changes fastest.
Arguments:
- inputs: float32 [16, 8, 64, 128], P(('grp', 'tm'), 'space'), parts along dimension 0, may hold values from -6 to 6
- pre_first: float32 [16, 8, 64, 128], P(('grp', 'tm'), 'space'), parts along dimension 0, may hold values from -8 to 8
- pre_second: float32 [16, 8, 64, 128], P(('grp', 'tm'), 'space'), parts along dimension 0, may hold values from -8 to 8
- cotangent: float32 [16, 8, 64, 128], P(('grp', 'tm'), 'space'), parts along dimension 0, may hold values from -6 to 6
- weight_first: float32 [27, 128, 128], P(None, 'space'), may hold values from -0.109375 to 0.109375
- weight_second: float32 [27, 128, 128], P(None, 'space'), may hold values from -0.109375 to 0.109375
- clip_lengths: int32 [8], P('grp'), parts along dimension 0, may hold values from 1 to 4, as said below
Outputs:
- grad_inputs: float32 [16, 8, 64, 128], P(('grp', 'tm'), 'space'), parts along dimension 0
- grad_first: float32 [54, 128, 128], P('grp', 'space'), parts along dimension 0
- grad_second: float32 [54, 128, 128], P('grp', 'space'), parts along dimension 0
There are 2 independent parts, one for each index of `grp`. A program takes and returns all parts, laid end to end along the dimension named above; an argument that names none is the same for every part. Nothing has to cross between parts.
Inputs may be any that keep to these rules, and one draw needn't show every extreme that they name: `clip_lengths`: the clip lengths sum to 8, and the longest is exactly 4.
All inputs are finite; a program needn't handle non-finite values.
Results may differ from a plain program's by a relative error of at most 0.0001.
Values sent between devices are 32-bit elements; how exact they have to be, the bound alone decides.
A program may use at most 64 MiB of HBM per device.

v0:
```python
import jax
import jax.numpy as jnp
from jax import lax
from jax.sharding import PartitionSpec as P


def from_behind(block, axis, distance):
    devices = range(lax.axis_size(axis))
    route = [(i - distance, i) for i in devices if i - distance in devices]
    return lax.ppermute(block, axis, route)


def extended(shard, sides, width):
    for axis, dim in sides:
        devices, length = (lax.axis_size(axis), shard.shape[dim])
        up = [(i, (i + 1) % devices) for i in range(devices - 1)]
        down = [(j, i) for i, j in up]
        last = lax.slice_in_dim(shard, length - width, length, axis=dim)
        leading = lax.slice_in_dim(shard, 0, width, axis=dim)
        before = lax.ppermute(last, axis, up)
        after = lax.ppermute(leading, axis, down)
        shard = jnp.concatenate([before, shard, after], axis=dim)
    return shard


def silu_slope(values):
    sigma = jax.nn.sigmoid(values)
    return sigma * (1.0 + values * (1.0 - sigma))


def clip_number(lengths, frames):
    endings = jnp.cumsum(lengths)
    return jnp.sum((endings[None, :] <= frames[:, None]).astype(jnp.int32), axis=1)


def masked_views(grad, lengths):
    frames = grad.shape[0]
    later = from_behind(grad, "tm", -1)
    longer = jnp.concatenate([grad, later], axis=0)
    padded = extended(longer, (("space", 1),), 1)
    padded = jnp.pad(padded, ((0, 0), (0, 0), (1, 1), (0, 0)))
    global_frames = lax.axis_index("tm") * frames + jnp.arange(frames + 2, dtype=jnp.int32)
    number = clip_number(lengths, global_frames)
    views = []
    for ahead in range(3):
        same = (number[ahead : ahead + frames] == number[:frames]).astype(jnp.float32)
        views.append(padded[ahead : ahead + frames] * same[:, None, None, None])
    return views


def window_of(views, tap_t, tap_h, tap_w, height, breadth):
    chans = views[0].shape[3]
    part = views[2 - tap_t][:, 2 - tap_h : 2 - tap_h + height, 2 - tap_w : 2 - tap_w + breadth, :]
    return part.reshape(-1, chans)


def kernel_terms(fields, views):
    height, breadth, chans = (fields.shape[1], fields.shape[2], fields.shape[3])
    flat = fields.reshape(-1, chans)
    taps_out = []
    for tap_t in range(3):
        for tap_h in range(3):
            for tap_w in range(3):
                part = window_of(views, tap_t, tap_h, tap_w, height, breadth)
                taps_out.append(
                    lax.dot_general(
                        flat, part, (((0,), (0,)), ((), ())), precision=lax.Precision.HIGHEST
                    )
                )
    return jnp.stack(taps_out)


def reduce_kernel(partial_value):
    whole = lax.psum(partial_value, "tm")
    return lax.psum_scatter(whole, "space", scatter_dimension=1, tiled=True)


def input_grad(views, weight, shape):
    frames, height, breadth = (shape[0], shape[1], shape[2])
    piece = lax.all_gather(weight, "space", axis=1, tiled=True)
    total = jnp.zeros((frames * height * breadth, piece.shape[1]), jnp.float32)
    for tap_t in range(3):
        for tap_h in range(3):
            for tap_w in range(3):
                part = window_of(views, tap_t, tap_h, tap_w, height, breadth)
                total = total + lax.dot_general(
                    part,
                    piece[9 * tap_t + 3 * tap_h + tap_w],
                    (((1,), (1,)), ((), ())),
                    precision=lax.Precision.HIGHEST,
                )
    return total.reshape(frames, height, breadth, piece.shape[1])


def shards(inputs, pre_first, pre_second, cotangent, weight_first, weight_second, clip_lengths):
    cells = (
        inputs.shape[0]
        * lax.axis_size("tm")
        * inputs.shape[1]
        * lax.axis_size("space")
        * inputs.shape[2]
    )
    factor = 1.0 / cells**0.5
    grad_second_pre = cotangent * silu_slope(pre_second)
    views_second = masked_views(grad_second_pre, clip_lengths)
    grad_second = reduce_kernel(kernel_terms(jax.nn.silu(pre_first), views_second) * factor)
    grad_hidden = input_grad(views_second, weight_second, inputs.shape)
    grad_first_pre = grad_hidden * silu_slope(pre_first)
    views_first = masked_views(grad_first_pre, clip_lengths)
    grad_first = reduce_kernel(kernel_terms(inputs, views_first) * factor)
    grad_inputs = input_grad(views_first, weight_first, inputs.shape)
    return (grad_inputs, grad_first, grad_second)


def solution(mesh):
    placed = (
        P(("grp", "tm"), "space", None, None),
        P(("grp", "tm"), "space", None, None),
        P(("grp", "tm"), "space", None, None),
        P(("grp", "tm"), "space", None, None),
        P(None, "space", None),
        P(None, "space", None),
        P("grp"),
    )
    return jax.shard_map(
        shards,
        mesh=mesh,
        in_specs=placed,
        out_specs=(
            P(("grp", "tm"), "space", None, None),
            P("grp", "space", None),
            P("grp", "space", None),
        ),
        check_vma=False,
    )
```

profile of v0, /device:TPU:0, one launch (start us, length us, event | category | flops | bytes accessed | tf_op | source)
XLA Modules:
  0.0 216.7 jit_solution(624966249513701505)
XLA Ops:
  9.0 1.3 collective-permute-start
  11.4 6.0 %collective-permute-done = f32[2,2,64,128]{3,2,1,0:T(8,128)S(1)} collective-permute-done((f32[2,2,64,128]{3,2,1,0:T(8,128)S(1)}, f32[2,2,64,128]{3,2,1,0:T(8,128)S(1)}, u32[]{:S(2)}, u32[]{:S(2)}) %collective-permute-start) | collective-permute-done | bytes 131104 | tf_op jit(solution)/shard_map/ppermute | solution.py:10
  17.4 1.3 collective-permute-start.1
  18.7 1.3 collective-permute-start.2
  20.1 3.7 %collective-permute-done.2 = f32[4,1,64,128]{3,2,1,0:T(8,128)S(1)} collective-permute-done((f32[4,1,64,128]{3,2,1,0:T(8,128)S(1)}, f32[4,1,64,128]{3,2,1,0:T(8,128)S(1)}, u32[]{:S(2)}, u32[]{:S(2)}) %collective-permute-start.2) | collective-permute-done | bytes 131104 | tf_op jit(solution)/shard_map/ppermute | solution.py:21
  52.2 1.3 fusion.77
  53.5 1.2 fusion.76
  54.8 1.2 convolution_add_fusion.47
  64.8 1.3 collective-permute-start.3
  67.2 4.5 %collective-permute-done.3 = f32[2,2,64,128]{3,2,1,0:T(8,128)S(1)} collective-permute-done((f32[2,2,64,128]{3,2,1,0:T(8,128)S(1)}, f32[2,2,64,128]{3,2,1,0:T(8,128)S(1)}, u32[]{:S(2)}, u32[]{:S(2)}) %collective-permute-start.3) | collective-permute-done | bytes 131104 | tf_op jit(solution)/shard_map/ppermute | solution.py:10
  71.7 7.4 %collective-permute-start.4 = (f32[4,1,64,128]{3,2,1,0:T(8,128)S(1)}, f32[4,1,64,128]{3,2,1,0:T(8,128)S(1)}, u32[]{:S(2)}, u32[]{:S(2)}) collective-permute-start(f32[4,1,64,128]{3,2,1,0:T(8,128)S(1)} %get-tuple-element.68), channel_id=1, source_target_pairs={{0,1},{1,2},{2,3},{4,5},{5,6},{6,7},{8,9},{9,10},{10,11},{12,13},{... | collective-permute-start | bytes 393224 | tf_op jit(solution)/shard_map/ppermute | solution.py:20
  79.2 1.3 collective-permute-start.5
  80.5 1.6 broadcast_multiply_fusion
  82.1 2.3 %copy.98 = f32[27,128,128]{2,0,1:T(8,128)} copy(f32[27,128,128]{1,2,0:T(8,128)S(1)} %broadcast_multiply_fusion) | data formatting | bytes 3538944 | tf_op jit(solution)/shard_map/mul | solution.py:106
  96.1 2.2 %copy.70 = f32[27,128,128]{2,0,1:T(8,128)} copy(f32[27,128,128]{1,2,0:T(8,128)S(1)} %broadcast_multiply_fusion.1) | data formatting | bytes 3538944 | tf_op jit(solution)/shard_map/mul | solution.py:110
  101.2 1.3 fusion.74
  102.6 1.3 convolution_add_fusion.23
  103.9 1.2 convolution_add_fusion.22
  105.1 1.2 convolution_add_fusion.21
  112.8 4.8 %reduce-scatter.5.cloned.1.call-done = f32[27,32,128]{2,0,1:T(8,128)} async-done(((f32[27,128,128]{2,0,1:T(8,128)}), f32[27,32,128]{2,0,1:T(8,128)}) %reduce-scatter.5.cloned.1.call-update) | async-done | bytes 442384 | tf_op jit(solution)/shard_map/reduce_scatter | solution.py:75
  117.6 34.0 %reduce-scatter.3.cloned.1.call-done = f32[27,32,128]{2,0,1:T(8,128)} async-done(((f32[27,128,128]{2,0,1:T(8,128)}), f32[27,32,128]{2,0,1:T(8,128)}) %reduce-scatter.3.cloned.1.call-update) | async-done | bytes 442384 | tf_op jit(solution)/shard_map/reduce_scatter | solution.py:75
  153.4 52.6 %all-reduce.5.cloned.1.call-done = (f32[27,32,128]{2,0,1:T(8,128)}, f32[27,32,128]{2,0,1:T(8,128)}) async-done(((f32[27,32,128]{2,0,1:T(8,128)}, f32[27,32,128]{2,0,1:T(8,128)}), (f32[27,32,128]{2,0,1:T(8,128)}, f32[27,32,128]{2,0,1:T(8,128)})) %all-reduce.5.cloned.1.call-update) | async-done | bytes 884752 | tf_op jit(solution)/shard_map/psum | solution.py:74
  206.0 2.1 copy.100
  208.1 2.1 copy.99
  (184 shorter events, 63.4 us)
Async XLA Ops:
  7.2 78.2 %copy-start = (f32[2,2,64,128]{3,2,1,0:T(8,128)S(1)}, f32[2,2,64,128]{3,2,1,0:T(8,128)}, u32[]{:S(2)}) copy-start(f32[2,2,64,128]{3,2,1,0:T(8,128)} %param.7) | copy-start | bytes 393220
  7.2 45.0 %all-gather.3.cloned.1.call-start = ((), (), s32[]{:S(2)}) async-start(), calls=%async_computation.2 | async-start | bytes 2211840 | tf_op jit(solution)/shard_map/all_gather | solution.py:80
  7.9 93.3 %all-gather.5.cloned.1.call-start = ((), (), s32[]{:S(2)}) async-start(), calls=%async_computation.3 | async-start | bytes 2211840 | tf_op jit(solution)/shard_map/all_gather | solution.py:80
  9.0 8.4 %collective-permute-start = (f32[2,2,64,128]{3,2,1,0:T(8,128)S(1)}, f32[2,2,64,128]{3,2,1,0:T(8,128)S(1)}, u32[]{:S(2)}, u32[]{:S(2)}) collective-permute-start(f32[2,2,64,128]{3,2,1,0:T(8,128)S(1)} %multiply_multiply_fusion.1), channel_id=1, source_target_pairs={{4,0},{8,4},{12,8},{5,1},{9,5},{13,9},{6,2},{10,6},{14,10},{7,3},{... | collective-permute-start | bytes 393224 | tf_op jit(solution)/shard_map/ppermute | solution.py:10
  10.3 107.3 %reduce-scatter.5.cloned.1.call-start = ((), (), s32[]{:S(2)}) async-start(), calls=%async_computation.5 | async-start | bytes 2621440 | tf_op jit(solution)/shard_map/reduce_scatter | solution.py:75
  17.4 2.7 %collective-permute-start.1 = (f32[4,1,64,128]{3,2,1,0:T(8,128)S(1)}, f32[4,1,64,128]{3,2,1,0:T(8,128)S(1)}, u32[]{:S(2)}, u32[]{:S(2)}) collective-permute-start(f32[4,1,64,128]{3,2,1,0:T(8,128)S(1)} %get-tuple-element.72), channel_id=1, source_target_pairs={{0,1},{1,2},{2,3},{4,5},{5,6},{6,7},{8,9},{9,10},{10,11},{12,13},{... | collective-permute-start | bytes 393224 | tf_op jit(solution)/shard_map/ppermute | solution.py:20
  18.7 5.1 %collective-permute-start.2 = (f32[4,1,64,128]{3,2,1,0:T(8,128)S(1)}, f32[4,1,64,128]{3,2,1,0:T(8,128)S(1)}, u32[]{:S(2)}, u32[]{:S(2)}) collective-permute-start(f32[4,1,64,128]{3,2,1,0:T(8,128)S(1)} %get-tuple-element.73), channel_id=1, source_target_pairs={{1,0},{2,1},{3,2},{5,4},{6,5},{7,6},{9,8},{10,9},{11,10},{13,12},{... | collective-permute-start | bytes 393224 | tf_op jit(solution)/shard_map/ppermute | solution.py:21
  45.1 6.1 %copy-start.19 = (f32[2,2,64,128]{3,2,1,0:T(8,128)}, f32[2,2,64,128]{3,2,1,0:T(8,128)S(1)}, u32[]{:S(2)}) copy-start(f32[2,2,64,128]{3,2,1,0:T(8,128)S(1)} %get-tuple-element.71) | copy-start | bytes 393220
  45.1 6.1 %copy-start.17 = (f32[2,2,64,128]{3,2,1,0:T(8,128)}, f32[2,2,64,128]{3,2,1,0:T(8,128)S(1)}, u32[]{:S(2)}) copy-start(f32[2,2,64,128]{3,2,1,0:T(8,128)S(1)} %get-tuple-element.70) | copy-start | bytes 393220
  48.1 7.8 %copy-start.10 = (f32[2,2,64,128]{3,2,1,0:T(8,128)S(1)}, f32[2,2,64,128]{3,2,1,0:T(8,128)}, u32[]{:S(2)}) copy-start(f32[2,2,64,128]{3,2,1,0:T(8,128)} %get-tuple-element.78) | copy-start | bytes 393220
  52.2 6.0 %copy-start.2 = (f32[27,128,128]{2,1,0:T(8,128)S(1)}, f32[27,128,128]{2,1,0:T(8,128)}, u32[]{:S(2)}) copy-start(f32[27,128,128]{2,1,0:T(8,128)} %all-gather.3.cloned.1.call-done) | copy-start | bytes 5308420
  64.8 6.9 %collective-permute-start.3 = (f32[2,2,64,128]{3,2,1,0:T(8,128)S(1)}, f32[2,2,64,128]{3,2,1,0:T(8,128)S(1)}, u32[]{:S(2)}, u32[]{:S(2)}) collective-permute-start(f32[2,2,64,128]{3,2,1,0:T(8,128)S(1)} %multiply_multiply_fusion), channel_id=1, source_target_pairs={{4,0},{8,4},{12,8},{5,1},{9,5},{13,9},{6,2},{10,6},{14,10},{7,3},{... | collective-permute-start | bytes 393224 | tf_op jit(solution)/shard_map/ppermute | solution.py:10
  71.7 12.7 %collective-permute-start.4 = (f32[4,1,64,128]{3,2,1,0:T(8,128)S(1)}, f32[4,1,64,128]{3,2,1,0:T(8,128)S(1)}, u32[]{:S(2)}, u32[]{:S(2)}) collective-permute-start(f32[4,1,64,128]{3,2,1,0:T(8,128)S(1)} %get-tuple-element.68), channel_id=1, source_target_pairs={{0,1},{1,2},{2,3},{4,5},{5,6},{6,7},{8,9},{9,10},{10,11},{12,13},{... | collective-permute-start | bytes 393224 | tf_op jit(solution)/shard_map/ppermute | solution.py:20
  79.2 5.3 %collective-permute-start.5 = (f32[4,1,64,128]{3,2,1,0:T(8,128)S(1)}, f32[4,1,64,128]{3,2,1,0:T(8,128)S(1)}, u32[]{:S(2)}, u32[]{:S(2)}) collective-permute-start(f32[4,1,64,128]{3,2,1,0:T(8,128)S(1)} %get-tuple-element.69), channel_id=1, source_target_pairs={{1,0},{2,1},{3,2},{5,4},{6,5},{7,6},{9,8},{10,9},{11,10},{13,12},{... | collective-permute-start | bytes 393224 | tf_op jit(solution)/shard_map/ppermute | solution.py:21
  84.4 67.1 %reduce-scatter.3.cloned.1.call-start = ((), (), s32[]{:S(2)}) async-start(), calls=%async_computation.4 | async-start | bytes 2621440 | tf_op jit(solution)/shard_map/reduce_scatter | solution.py:75
  100.2 6.1 %copy-start.12 = (f32[2,2,64,128]{3,2,1,0:T(8,128)S(1)}, f32[2,2,64,128]{3,2,1,0:T(8,128)}, u32[]{:S(2)}) copy-start(f32[2,2,64,128]{3,2,1,0:T(8,128)} %get-tuple-element.43) | copy-start | bytes 393220
  100.2 7.2 %copy-start.11 = (f32[2,2,64,128]{3,2,1,0:T(8,128)S(1)}, f32[2,2,64,128]{3,2,1,0:T(8,128)}, u32[]{:S(2)}) copy-start(f32[2,2,64,128]{3,2,1,0:T(8,128)} %get-tuple-element.42) | copy-start | bytes 393220
  100.2 105.8 %all-reduce.5.cloned.1.call-start = ((), (), s32[]{:S(2)}) async-start(), calls=%async_computation.6 | async-start | bytes 2097152 | tf_op jit(solution)/shard_map/psum | solution.py:74
  101.2 6.1 %copy-start.1 = (f32[27,128,128]{2,1,0:T(8,128)S(1)}, f32[27,128,128]{2,1,0:T(8,128)}, u32[]{:S(2)}) copy-start(f32[27,128,128]{2,1,0:T(8,128)} %all-gather.5.cloned.1.call-done) | copy-start | bytes 5308420
  102.6 6.0 %copy-start.15 = (f32[2,2,64,128]{3,2,1,0:T(8,128)S(1)}, f32[2,2,64,128]{3,2,1,0:T(8,128)}, u32[]{:S(2)}) copy-start(f32[2,2,64,128]{3,2,1,0:T(8,128)} %get-tuple-element.17) | copy-start | bytes 393220
  111.3 40.3 %copy-start.14 = (f32[2,2,64,128]{3,2,1,0:T(8,128)S(1)}, f32[2,2,64,128]{3,2,1,0:T(8,128)}, u32[]{:S(2)}) copy-start(f32[2,2,64,128]{3,2,1,0:T(8,128)} %get-tuple-element.19) | copy-start | bytes 393220
  111.6 40.3 %copy-start.7 = (f32[2,2,64,128]{3,2,1,0:T(8,128)S(1)}, f32[2,2,64,128]{3,2,1,0:T(8,128)}, u32[]{:S(2)}) copy-start(f32[2,2,64,128]{3,2,1,0:T(8,128)} %get-tuple-element.15) | copy-start | bytes 393220
  111.9 40.3 %copy-start.6 = (f32[2,2,64,128]{3,2,1,0:T(8,128)S(1)}, f32[2,2,64,128]{3,2,1,0:T(8,128)}, u32[]{:S(2)}) copy-start(f32[2,2,64,128]{3,2,1,0:T(8,128)} %get-tuple-element.14) | copy-start | bytes 393220
  111.9 40.6 %copy-start.16 = (f32[2,2,64,128]{3,2,1,0:T(8,128)S(1)}, f32[2,2,64,128]{3,2,1,0:T(8,128)}, u32[]{:S(2)}) copy-start(f32[2,2,64,128]{3,2,1,0:T(8,128)} %get-tuple-element.66) | copy-start | bytes 393220
  (11 other events, 26.7 us)
Sparse Core Ops, SparseCore 0:
  9.6 24.8 all-gather.2
  36.0 20.7 all-gather.4
  84.5 33.0 reduce-scatter.4
  120.1 31.3 reduce-scatter.2
  153.8 52.1 all-reduce.4
where the time goes:
time: 217 us
  waiting for transfers between devices  106 us (49%)
  matrix products  63 us (29%)
  between operations  14.8 us (7%)
  starting transfers between devices  14.3 us (7%)
  local copies, waits for them, and re-layouts  13.1 us (6%)
  other arithmetic  5.05 us (2%)
    psum x1, waiting for transfers between devices, reduce_kernel(): whole = lax.psum(partial_value, 'tm')  52.6 us
    reduce_scatter x2, waiting for transfers between devices, reduce_kernel(): return lax.psum_scatter(whole, 'space', scatter_dimension=1, tiled=True)  38.8 us
    dot_general x54, matrix products, kernel_terms(): lax.dot_general(flat, part, (((0,), (0,)), ((), ())), precision=lax.Preci...  37.9 us
    dot_general x54, matrix products, input_grad(): lax.dot_general(part, piece[9 * tap_t + 3 * tap_h + tap_w], (((1,), (1,))...  25.1 us
    ppermute x2, waiting for transfers between devices, from_behind(): return lax.ppermute(block, axis, route)  10.6 us
    ppermute x2, starting transfers between devices, extended(): before = lax.ppermute(last, axis, up)  8.73 us
    unnamed x50, local copies, waits for them, and re-layouts  4.88 us
  transfers between devices with their start and end apart: 11, of which 6 were waited for; matrix products, arithmetic and copies ran while one was open for 35% of the time, Pallas kernels for 0%

commit v1 on v0

v1 whole, which is shorter than its diff:
```python
import functools
import itertools

import jax
import jax.numpy as jnp
from jax import lax
from jax.experimental import pallas as pl
from jax.experimental.pallas import tpu as pltpu
from jax.sharding import PartitionSpec as P

F32 = jnp.float32
BF16 = jnp.bfloat16


def silu_slope(values):
    sigma = 1.0 / (1.0 + jnp.exp(-values))
    return sigma * (1.0 + values * (1.0 - sigma))


def halves(values):
    high = values.astype(BF16)
    low = (values - high.astype(F32)).astype(BF16)
    return high, low


def kernel(
    dims,
    x_ref, p1_ref, p2_ref, ct_ref, w1_ref, w2_ref, len_ref,
    gi_ref, g1_ref, g2_ref,
    rows_buf, chan_buf, xp, xr, pp, pr, op, orr,
    gb2, gb1, wb2, wb1, ft2, ft1,
    part2, part1, rs2, rs1, full2, full1,
    send_sem, recv_sem,
):
    S, T, F, R, W, C, CI, NC, MP, B = dims
    X = S // 2
    H = S * R
    J = F * R
    tm = lax.axis_index("tm")
    s = lax.axis_index("space")
    core = lax.rem(s, 2)
    xi = s // 2
    sib = s + 1 - 2 * core
    count = itertools.count()
    sent = []

    def xpeer(d):
        return lax.rem(xi + d, X) * 2 + core

    def copy(src, dst, **target):
        i = next(count)
        c = pltpu.make_async_remote_copy(
            src_ref=src, dst_ref=dst, send_sem=send_sem.at[i], recv_sem=recv_sem.at[i],
            device_id=target, device_id_type=pl.DeviceIdType.MESH,
        )
        c.start()
        sent.append(c)
        return c

    def pack(pieces):
        tail = 128 - J * CI
        if tail:
            pieces = pieces + [jnp.zeros((W, tail), F32)]
        return jnp.concatenate(pieces, axis=1)

    barrier = pltpu.get_barrier_semaphore()
    for d in range(1, S):
        pl.semaphore_signal(barrier, inc=1, device_id={"space": lax.rem(s + d, S)}, device_id_type=pl.DeviceIdType.MESH)
    for d in range(1, T):
        pl.semaphore_signal(barrier, inc=1, device_id={"tm": lax.rem(tm + d, T)}, device_id_type=pl.DeviceIdType.MESH)

    ends = []
    run = jnp.int32(0)
    for j in range(NC):
        run = run + len_ref[j]
        ends.append(run)
    number = []
    for a in range(F + 2):
        frame = tm * F + a
        n = jnp.int32(0)
        for e in ends:
            n = n + jnp.where(e <= frame, jnp.int32(1), jnp.int32(0))
        number.append(n)
    mask = [[jnp.where(number[f + a] == number[f], F32(1.0), F32(0.0)) for a in range(3)] for f in range(F)]

    rows_buf[0, s] = ct_ref[...] * silu_slope(p2_ref[...])
    for b in range(S):
        pp[b] = pack([p1_ref[j * W:(j + 1) * W, b * CI:(b + 1) * CI] for j in range(J)])
    pl.semaphore_wait(barrier, S - 1 + T - 1)

    def spread(buf, half):
        near = copy(buf.at[half, s], buf.at[half, s], space=sib)
        far = [copy(buf.at[half, s], buf.at[half, s], space=xpeer(d)) for d in range(1, X)]
        return near, far

    def relay(buf, half, far):
        out = []
        for d in range(1, X):
            far[d - 1].wait_recv()
            origin = xpeer(X - d)
            out.append(copy(buf.at[half, origin], buf.at[half, origin], space=sib))
        return out

    def send_all(buf):
        back = copy(buf.at[0, s], buf.at[1, s], tm=lax.rem(tm + T - 1, T))
        near, far = spread(buf, 0)
        return back, near, far

    def exchange(src, dst):
        return [copy(src.at[lax.rem(s + d, S)], dst.at[s], space=lax.rem(s + d, S)) for d in range(1, S)]

    back, near, far = send_all(rows_buf)
    pcopies = exchange(pp, pr)
    pr[s] = pp[s]
    for b in range(S):
        xp[b] = pack([x_ref[j * W:(j + 1) * W, b * CI:(b + 1) * CI] for j in range(J)])
    xcopies = exchange(xp, xr)
    xr[s] = xp[s]

    def weights(w_ref, wb):
        wb[...] = jnp.zeros_like(wb)
        for kt in range(3):
            for kh in range(3):
                at = (3 * kt + kh) * 3 * CI
                high, low = halves(w_ref[at:at + 3 * CI, :])
                for dup in range(2):
                    c0 = kh * 2 * C + dup * C
                    wb[kt, 0:3 * CI, c0:c0 + C] = high
                    wb[kt, 128:128 + 3 * CI, c0:c0 + C] = low

    weights(w2_ref, wb2)
    for gb in (gb2, gb1):
        gb[:, 0] = jnp.zeros((2 * F, W, 2 * C), BF16)
        gb[:, H + 1] = jnp.zeros((2 * F, W, 2 * C), BF16)

    def finish(buf, back, near, far):
        out = relay(buf, 0, far)
        back.wait_recv()
        near1, far1 = spread(buf, 1)
        out += relay(buf, 1, far1)
        for c in [near, near1] + out:
            c.wait_recv()

    finish(rows_buf, back, near, far)
    for half in range(2):
        for b in range(S):
            for f in range(F):
                for r in range(R):
                    at = (f * R + r) * W
                    high, low = halves(rows_buf[half, b, at:at + W, :])
                    gb2[half * F + f, 1 + b * R + r, :, 0:C] = high
                    gb2[half * F + f, 1 + b * R + r, :, C:2 * C] = low

    pos = lax.rem(lax.broadcasted_iota(jnp.int32, (H * W, 128), 0), W)

    def input_grad(gb, wb):
        result = []
        for f in range(F):
            acc = None
            for kt in range(3):
                a = 2 - kt
                view = jnp.concatenate(
                    [gb[f + a, 2 - kh:2 - kh + H].reshape(H * W, 2 * C) for kh in range(3)], axis=1
                )
                d = lax.dot_general(view, wb[kt], (((1,), (1,)), ((), ())), preferred_element_type=F32)
                d = (d[:, 0:128] + d[:, 128:256]) * mask[f][a]
                acc = d if acc is None else acc + d
            up = jnp.where(pos == W - 1, 0.0, pltpu.roll(acc, H * W - 1, 0))
            down = jnp.where(pos == 0, 0.0, pltpu.roll(acc, 1, 0))
            result.append(up[:, 0:CI] + acc[:, CI:2 * CI] + down[:, 2 * CI:3 * CI])
        return result

    def packed_rows(parts, b):
        return pack([parts[f][(b * R + r) * W:(b * R + r + 1) * W, :] for f in range(F) for r in range(R)])

    hidden = input_grad(gb2, wb2)
    for c in pcopies:
        c.wait_recv()
    for b in range(S):
        chan_buf[0, s, b * W:(b + 1) * W, :] = packed_rows(hidden, b) * silu_slope(pr[b])
    back, near, far = send_all(chan_buf)

    wpos = lax.broadcasted_iota(jnp.int32, (W, 128), 0)

    def turned(fields, ft):
        cols = [[] for _ in range(F)]
        for b in range(S):
            mid = fields(b)
            down = jnp.where(wpos == 0, 0.0, pltpu.roll(mid, 1, 0))
            up = jnp.where(wpos == W - 1, 0.0, pltpu.roll(mid, W - 1, 0))
            for f in range(F):
                for r in range(R):
                    j = f * R + r
                    cols[f].append(jnp.concatenate(
                        [v[:, j * CI:(j + 1) * CI] for v in (down, mid, up)]
                        + [jnp.zeros((W, 128 - 3 * CI), F32)], axis=1))
        for f in range(F):
            whole = jnp.concatenate(cols[f], axis=0).T
            high, low = halves(whole[0:MP])
            ft[f, 0:MP] = high
            ft[f, MP:2 * MP] = low

    def kernel_grad(gb, ft, part):
        for kt in range(3):
            a = 2 - kt
            for kh in range(3):
                acc = None
                for f in range(F):
                    view = gb[f + a, 2 - kh:2 - kh + H].reshape(H * W, 2 * C)
                    d = jnp.dot(ft[f], view, preferred_element_type=F32)
                    d = (d[0:MP, 0:C] + d[MP:2 * MP, 0:C] + d[0:MP, C:2 * C]) * mask[f][a]
                    acc = d if acc is None else acc + d
                at = (3 * kt + kh) * 3 * CI
                part[at:at + 3 * CI, :] = acc[0:3 * CI]

    def silu(v):
        return v / (1.0 + jnp.exp(-v))

    def scatter(part, rs):
        out = []
        for d in range(1, T):
            to = lax.rem(tm + d, T)
            out.append(copy(part.at[pl.ds(pl.multiple_of(to * B, 8), B)], rs.at[tm], tm=to))
        return out

    scale = 1.0 / (F * T * H * W) ** 0.5

    def gather(copies, part, rs, full):
        for c in copies:
            c.wait_recv()
        mine = pl.ds(pl.multiple_of(tm * B, 8), B)
        total = part[mine, :]
        for d in range(1, T):
            total = total + rs[lax.rem(tm + d, T)]
        full[mine, :] = total * scale
        return [copy(full.at[mine], full.at[mine], tm=lax.rem(tm + d, T)) for d in range(1, T)]

    if T * B > 27 * CI:
        for part in (part2, part1):
            part[27 * CI:T * B, :] = jnp.zeros((T * B - 27 * CI, C), F32)

    turned(lambda b: silu(pr[b]), ft2)
    kernel_grad(gb2, ft2, part2)
    weights(w1_ref, wb1)
    finish(chan_buf, back, near, far)
    red2 = scatter(part2, rs2)
    for half in range(2):
        for b in range(S):
            for f in range(F):
                for r in range(R):
                    j = f * R + r
                    value = jnp.concatenate(
                        [chan_buf[half, q, b * W:(b + 1) * W, j * CI:(j + 1) * CI] for q in range(S)], axis=1)
                    high, low = halves(value)
                    gb1[half * F + f, 1 + b * R + r, :, 0:C] = high
                    gb1[half * F + f, 1 + b * R + r, :, C:2 * C] = low
    for c in xcopies:
        c.wait_recv()
    turned(lambda b: xr[b], ft1)
    kernel_grad(gb1, ft1, part1)
    red1 = scatter(part1, rs1)
    result = input_grad(gb1, wb1)
    for b in range(S):
        op[b] = packed_rows(result, b)
    ocopies = exchange(op, orr)
    orr[s] = op[s]
    all2 = gather(red2, part2, rs2, full2)
    all1 = gather(red1, part1, rs1, full1)
    for c in ocopies:
        c.wait_recv()
    for f in range(F):
        for r in range(R):
            j = f * R + r
            gi_ref[j * W:(j + 1) * W, :] = jnp.concatenate(
                [orr[q, :, j * CI:(j + 1) * CI] for q in range(S)], axis=1)
    for c in all2:
        c.wait_recv()
    g2_ref[...] = full2[0:27 * CI, :]
    for c in all1:
        c.wait_recv()
    g1_ref[...] = full1[0:27 * CI, :]
    for c in sent:
        c.wait_send()


def shards(S, T, inputs, pre_first, pre_second, cotangent, weight_first, weight_second, clip_lengths):
    F, R, W, C = inputs.shape
    CI = weight_first.shape[1]
    NC = clip_lengths.shape[0]
    X = S // 2
    H = S * R
    cells = F * R * W
    MP = -(-3 * CI // 16) * 16
    B = -(-27 * CI // (8 * T)) * 8
    n_sem = 2 * (1 + 2 * (1 + 2 * (X - 1))) + 3 * (S - 1) + 4 * (T - 1)
    dims = (S, T, F, R, W, C, CI, NC, MP, B)
    flat = lambda a: a.reshape(-1, a.shape[-1])
    vm = pl.BlockSpec(memory_space=pltpu.VMEM)
    piece = pltpu.VMEM((S, W, 128), F32)
    grad = pltpu.VMEM((T * B, C), F32)
    gi, g1, g2 = pl.pallas_call(
        functools.partial(kernel, dims),
        out_shape=(
            jax.ShapeDtypeStruct((cells, C), F32),
            jax.ShapeDtypeStruct((27 * CI, C), F32),
            jax.ShapeDtypeStruct((27 * CI, C), F32),
        ),
        in_specs=[vm] * 6 + [pl.BlockSpec(memory_space=pltpu.SMEM)],
        out_specs=(vm, vm, vm),
        scratch_shapes=[
            pltpu.VMEM((2, S, cells, C), F32),
            pltpu.VMEM((2, S, S * W, 128), F32),
            piece, piece, piece, piece, piece, piece,
            pltpu.VMEM((2 * F, H + 2, W, 2 * C), BF16),
            pltpu.VMEM((2 * F, H + 2, W, 2 * C), BF16),
            pltpu.VMEM((3, 256, 6 * C), BF16),
            pltpu.VMEM((3, 256, 6 * C), BF16),
            pltpu.VMEM((F, 2 * MP, H * W), BF16),
            pltpu.VMEM((F, 2 * MP, H * W), BF16),
            grad, grad,
            pltpu.VMEM((T, B, C), F32),
            pltpu.VMEM((T, B, C), F32),
            grad, grad,
            pltpu.SemaphoreType.DMA((n_sem,)),
            pltpu.SemaphoreType.DMA((n_sem,)),
        ],
        compiler_params=pltpu.CompilerParams(
            collective_id=0, has_side_effects=True, vmem_limit_bytes=56 * 1024 * 1024
        ),
    )(flat(inputs), flat(pre_first), flat(pre_second), flat(cotangent), flat(weight_first), flat(weight_second), clip_lengths)
    return gi.reshape(inputs.shape), g1.reshape(27, CI, C), g2.reshape(27, CI, C)


def solution(mesh):
    placed = (
        P(("grp", "tm"), "space", None, None),
        P(("grp", "tm"), "space", None, None),
        P(("grp", "tm"), "space", None, None),
        P(("grp", "tm"), "space", None, None),
        P(None, "space", None),
        P(None, "space", None),
        P("grp"),
    )
    return jax.shard_map(
        functools.partial(shards, mesh.shape["space"], mesh.shape["tm"]),
        mesh=mesh,
        in_specs=placed,
        out_specs=(
            P(("grp", "tm"), "space", None, None),
            P("grp", "space", None),
            P("grp", "space", None),
        ),
        check_vma=False,
    )
```

time: 217 us -> 74.3 us (0.34)
  waiting for transfers between devices: 106 us -> 0 us
  Pallas kernels: 0 us -> 69.1 us
  matrix products: 63 us -> 0 us
  starting transfers between devices: 14.3 us -> 0 us
  between operations: 14.8 us -> 0.64 us
  local copies, waits for them, and re-layouts: 13.1 us -> 4.19 us
  other arithmetic: 5.05 us -> 0 us
    pallas_call x0 -> x1, Pallas kernels: none -> 69.1 us  [shards(): pl.pallas_call(functools.partial(kernel, dims), out_shape=(jax.ShapeDtype...]
    dot_general x108 -> x0, matrix products: 63 us -> none  [the longest x54 37.9 us: kernel_terms(): lax.dot_general(flat, part, (((0,), (0,)), ((), ())), precision=lax.Preci...]
    psum x1 -> x0, waiting for transfers between devices: 52.6 us -> none  [reduce_kernel(): whole = lax.psum(partial_value, 'tm')]
    reduce_scatter x2 -> x0, waiting for transfers between devices: 38.8 us -> none  [reduce_kernel(): return lax.psum_scatter(whole, 'space', scatter_dimension=1, tiled=True)]
    ppermute x6 -> x0, waiting for transfers between devices: 14.3 us -> none  [the longest x2 10.6 us: from_behind(): return lax.ppermute(block, axis, route)]
    ppermute x6 -> x0, starting transfers between devices: 13.9 us -> none  [the longest x2 8.73 us: extended(): before = lax.ppermute(last, axis, up)]
    mul x2 -> x0, local copies, waits for them, and re-layouts: 4.55 us -> none  [the longest x1 2.31 us: shards(): kernel_terms(jax.nn.silu(pre_first), views_second) * factor]
    slice x5 -> x0, local copies, waits for them, and re-layouts: 3.64 us -> none  [window_of(): views[2 - tap_t]]
  transfers between devices with their start and end apart: 11 -> 0, of which waited for: 6 -> 0; matrix products, arithmetic and copies ran while one was open for 35% -> 0% of each run, Pallas kernels for 0% -> 0%
where the time goes in v1:
time: 74.3 us; the launch traced here: 73.9 us
  Pallas kernels  69.1 us (93%)
  local copies, waits for them, and re-layouts  4.19 us (6%)
    pallas_call x1, Pallas kernels, shards(): pl.pallas_call(functools.partial(kernel, dims), out_shape=(jax.ShapeDtype...  69.1 us
    unnamed x5, local copies, waits for them, and re-layouts  4.19 us

profile of v1, /device:TPU:0, one launch (start us, length us, event | category | flops | bytes accessed | tf_op | source)
XLA Modules:
  0.0 73.9 jit_solution(5760734681585069073)
XLA Ops:
  0.6 69.1 %shard_map.94 = (f32[256,128]{1,0:T(8,128)}, f32[864,128]{1,0:T(8,128)}, f32[864,128]{1,0:T(8,128)}) custom-call(f32[256,128]{1,0:T(8,128)} %bitcast.13, f32[256,128]{1,0:T(8,128)} %bitcast.14, f32[256,128]{1,0:T(8,128)} %bitcast.15, f32[256,128]{1,0:T(8,128)} %bitcast.16, f32[864,128]{1,0:T(8,128)} %bitcast.9, f32[864,128]{1,0:T(8,128)} %bitcast.10, s32[4]{0:T(128)} %len_ref.1), custom_call_target="tpu_custom_call" | custom-call | tf_op jit(solution)/shard_map/pallas_call | solution.py:301
  69.7 1.6 %copy.13 = f32[2,2,64,128]{3,2,1,0:T(8,128)} copy(f32[2,2,64,128]{3,2,1,0:T(8,128)} %bitcast.17) | data formatting | bytes 262144
  71.3 0.0 copy-start
  71.3 1.9 %copy.14 = f32[27,32,128]{2,1,0:T(8,128)} copy(f32[27,32,128]{2,1,0:T(8,128)} %bitcast.12) | data formatting | bytes 884736
  73.1 0.0 copy-done
  73.1 0.8 %copy.15 = f32[27,32,128]{2,1,0:T(8,128)} copy(f32[27,32,128]{2,1,0:T(8,128)S(1)} %bitcast.11) | data formatting | bytes 884736
Async XLA Ops:
  71.3 1.9 %copy-start = (f32[864,128]{1,0:T(8,128)S(1)}, f32[864,128]{1,0:T(8,128)}, u32[]{:S(2)}) copy-start(f32[864,128]{1,0:T(8,128)} %get-tuple-element.8) | copy-start | bytes 1327108

commit v2 on v1

--- a/solution.py
+++ b/solution.py
@@ -30,7 +30,7 @@
     rows_buf, chan_buf, xp, xr, pp, pr, op, orr,
     gb2, gb1, wb2, wb1, ft2, ft1,
     part2, part1, rs2, rs1, full2, full1,
-    send_sem, recv_sem,
+    send_sem, recv_sem, line_send, line_recv,
 ):
     S, T, F, R, W, C, CI, NC, MP, B = dims
     X = S // 2
@@ -101,20 +101,37 @@
             out.append(copy(buf.at[half, origin], buf.at[half, origin], space=sib))
         return out
 
-    def send_all(buf):
-        back = copy(buf.at[0, s], buf.at[1, s], tm=lax.rem(tm + T - 1, T))
-        near, far = spread(buf, 0)
-        return back, near, far
+    after = lax.rem(tm + 1, T)
+    before = lax.rem(tm + T - 1, T)
+
+    def hop(g, stage, way, t, src, dst):
+        return pltpu.make_async_remote_copy(
+            src_ref=src, dst_ref=dst,
+            send_sem=line_send.at[g, stage, way, t], recv_sem=line_recv.at[g, stage, way, t],
+            device_id={"tm": before if way else after}, device_id_type=pl.DeviceIdType.MESH,
+        )
+
+    def halo(g, buf):
+        return hop(g, 2, 1, 0, buf.at[0, s], buf.at[1, s])
+
+    def send_all(g, buf):
+        @pl.when(tm > 0)
+        def _():
+            halo(g, buf).start()
+
+        @pl.when(tm == T - 1)
+        def _():
+            buf[1, s] = jnp.zeros(buf.shape[2:], F32)
+
+        return spread(buf, 0)
 
     def exchange(src, dst):
         return [copy(src.at[lax.rem(s + d, S)], dst.at[s], space=lax.rem(s + d, S)) for d in range(1, S)]
 
-    back, near, far = send_all(rows_buf)
-    pcopies = exchange(pp, pr)
+    near, far = send_all(0, rows_buf)
     pr[s] = pp[s]
     for b in range(S):
         xp[b] = pack([x_ref[j * W:(j + 1) * W, b * CI:(b + 1) * CI] for j in range(J)])
-    xcopies = exchange(xp, xr)
     xr[s] = xp[s]
 
     def weights(w_ref, wb):
@@ -133,15 +150,21 @@
         gb[:, 0] = jnp.zeros((2 * F, W, 2 * C), BF16)
         gb[:, H + 1] = jnp.zeros((2 * F, W, 2 * C), BF16)
 
-    def finish(buf, back, near, far):
+    def finish(g, buf, near, far, between):
+        @pl.when(tm < T - 1)
+        def _():
+            halo(g, buf).wait_recv()
+
+        near1, far1 = spread(buf, 1)
         out = relay(buf, 0, far)
-        back.wait_recv()
-        near1, far1 = spread(buf, 1)
+        more = between()
         out += relay(buf, 1, far1)
         for c in [near, near1] + out:
             c.wait_recv()
-
-    finish(rows_buf, back, near, far)
+        return more
+
+    pcopies = finish(0, rows_buf, near, far, lambda: exchange(pp, pr))
+    xcopies = exchange(xp, xr)
     for half in range(2):
         for b in range(S):
             for f in range(F):
@@ -178,7 +201,7 @@
         c.wait_recv()
     for b in range(S):
         chan_buf[0, s, b * W:(b + 1) * W, :] = packed_rows(hidden, b) * silu_slope(pr[b])
-    back, near, far = send_all(chan_buf)
+    near, far = send_all(1, chan_buf)
 
     wpos = lax.broadcasted_iota(jnp.int32, (W, 128), 0)
 
@@ -216,24 +239,99 @@
     def silu(v):
         return v / (1.0 + jnp.exp(-v))
 
-    def scatter(part, rs):
-        out = []
-        for d in range(1, T):
-            to = lax.rem(tm + d, T)
-            out.append(copy(part.at[pl.ds(pl.multiple_of(to * B, 8), B)], rs.at[tm], tm=to))
-        return out
+    def block(ref, t):
+        return ref.at[pl.ds(pl.multiple_of(t * B, 8), B)]
+
+    def sum_hop(g, way, t, part, rs):
+        return hop(g, 0, way, t, block(part, t), rs.at[way, t])
+
+    def scatter_first(g, part, rs):
+        @pl.when(tm == 0)
+        def _():
+            for t in range(T - 1, 0, -1):
+                sum_hop(g, 0, t, part, rs).start()
+
+        @pl.when(tm == T - 1)
+        def _():
+            for t in range(T - 1):
+                sum_hop(g, 1, t, part, rs).start()
+
+    def scatter_middle(g, part, rs):
+        for k in range(T - 2):
+            for way, t in ((0, T - 1 - k), (1, k)):
+                inner = (tm > 0) & (tm < t) if way == 0 else (tm < T - 1) & (tm > t)
+
+                @pl.when(inner)
+                def _(way=way, t=t):
+                    c = sum_hop(g, way, t, part, rs)
+                    c.wait_recv()
+                    part[t * B:(t + 1) * B, :] += rs[way, t]
+                    c.start()
 
     scale = 1.0 / (F * T * H * W) ** 0.5
 
-    def gather(copies, part, rs, full):
-        for c in copies:
-            c.wait_recv()
+    def full_hop(g, way, t, full):
+        return hop(g, 1, way, t, block(full, t), block(full, t))
+
+    def own_block(g, part, rs, full):
         mine = pl.ds(pl.multiple_of(tm * B, 8), B)
-        total = part[mine, :]
-        for d in range(1, T):
-            total = total + rs[lax.rem(tm + d, T)]
-        full[mine, :] = total * scale
-        return [copy(full.at[mine], full.at[mine], tm=lax.rem(tm + d, T)) for d in range(1, T)]
+        for way, has in ((0, tm > 0), (1, tm < T - 1)):
+            @pl.when(has)
+            def _(way=way):
+                sum_hop(g, way, tm, part, rs).wait_recv()
+                part[mine, :] += rs[way, tm]
+
+        full[mine, :] = part[mine, :] * scale
+
+        @pl.when(tm < T - 1)
+        def _():
+            full_hop(g, 0, tm, full).start()
+
+        @pl.when(tm > 0)
+        def _():
+            full_hop(g, 1, tm, full).start()
+
+    def pass_on(g, full):
+        for k in range(1, T):
+            @pl.when(tm - k >= 0)
+            def _(k=k):
+                c = full_hop(g, 0, tm - k, full)
+                c.wait_recv()
+
+                @pl.when(tm < T - 1)
+                def _():
+                    c.start()
+
+            @pl.when(tm + k < T)
+            def _(k=k):
+                c = full_hop(g, 1, tm + k, full)
+                c.wait_recv()
+
+                @pl.when(tm > 0)
+                def _():
+                    c.start()
+
+    def settle(g, buf, part, rs, full):
+        @pl.when(tm > 0)
+        def _():
+            halo(g, buf).wait_send()
+
+        for t in range(T):
+            @pl.when((t > tm) & (tm < T - 1))
+            def _(t=t):
+                sum_hop(g, 0, t, part, rs).wait_send()
+
+            @pl.when((t < tm) & (tm > 0))
+            def _(t=t):
+                sum_hop(g, 1, t, part, rs).wait_send()
+
+            @pl.when((t <= tm) & (tm < T - 1))
+            def _(t=t):
+                full_hop(g, 0, t, full).wait_send()
+
+            @pl.when((t >= tm) & (tm > 0))
+            def _(t=t):
+                full_hop(g, 1, t, full).wait_send()
 
     if T * B > 27 * CI:
         for part in (part2, part1):
@@ -241,9 +339,9 @@
 
     turned(lambda b: silu(pr[b]), ft2)
     kernel_grad(gb2, ft2, part2)
+    scatter_first(0, part2, rs2)
     weights(w1_ref, wb1)
-    finish(chan_buf, back, near, far)
-    red2 = scatter(part2, rs2)
+    finish(1, chan_buf, near, far, lambda: scatter_middle(0, part2, rs2))
     for half in range(2):
         for b in range(S):
             for f in range(F):
@@ -258,14 +356,17 @@
         c.wait_recv()
     turned(lambda b: xr[b], ft1)
     kernel_grad(gb1, ft1, part1)
-    red1 = scatter(part1, rs1)
+    scatter_first(1, part1, rs1)
+    own_block(0, part2, rs2, full2)
     result = input_grad(gb1, wb1)
     for b in range(S):
         op[b] = packed_rows(result, b)
     ocopies = exchange(op, orr)
     orr[s] = op[s]
-    all2 = gather(red2, part2, rs2, full2)
-    all1 = gather(red1, part1, rs1, full1)
+    scatter_middle(1, part1, rs1)
+    pass_on(0, full2)
+    own_block(1, part1, rs1, full1)
+    g2_ref[...] = full2[0:27 * CI, :]
     for c in ocopies:
         c.wait_recv()
     for f in range(F):
@@ -273,12 +374,10 @@
             j = f * R + r
             gi_ref[j * W:(j + 1) * W, :] = jnp.concatenate(
                 [orr[q, :, j * CI:(j + 1) * CI] for q in range(S)], axis=1)
-    for c in all2:
-        c.wait_recv()
-    g2_ref[...] = full2[0:27 * CI, :]
-    for c in all1:
-        c.wait_recv()
+    pass_on(1, full1)
     g1_ref[...] = full1[0:27 * CI, :]
+    settle(0, rows_buf, part2, rs2, full2)
+    settle(1, chan_buf, part1, rs1, full1)
     for c in sent:
         c.wait_send()
 
@@ -292,7 +391,7 @@
     cells = F * R * W
     MP = -(-3 * CI // 16) * 16
     B = -(-27 * CI // (8 * T)) * 8
-    n_sem = 2 * (1 + 2 * (1 + 2 * (X - 1))) + 3 * (S - 1) + 4 * (T - 1)
+    n_sem = 4 * (1 + 2 * (X - 1)) + 3 * (S - 1)
     dims = (S, T, F, R, W, C, CI, NC, MP, B)
     flat = lambda a: a.reshape(-1, a.shape[-1])
     vm = pl.BlockSpec(memory_space=pltpu.VMEM)
@@ -318,11 +417,13 @@
             pltpu.VMEM((F, 2 * MP, H * W), BF16),
             pltpu.VMEM((F, 2 * MP, H * W), BF16),
             grad, grad,
-            pltpu.VMEM((T, B, C), F32),
-            pltpu.VMEM((T, B, C), F32),
+            pltpu.VMEM((2, T, B, C), F32),
+            pltpu.VMEM((2, T, B, C), F32),
             grad, grad,
             pltpu.SemaphoreType.DMA((n_sem,)),
             pltpu.SemaphoreType.DMA((n_sem,)),
+            pltpu.SemaphoreType.DMA((2, 3, 2, T)),
+            pltpu.SemaphoreType.DMA((2, 3, 2, T)),
         ],
         compiler_params=pltpu.CompilerParams(
             collective_id=0, has_side_effects=True, vmem_limit_bytes=56 * 1024 * 1024

time: 74.3 us -> 75.6 us (1.017)
  Pallas kernels: 69.1 us -> 70.6 us
    pallas_call x1, Pallas kernels: 69.1 us -> 70.6 us  [shards(): pl.pallas_call(functools.partial(kernel, dims), out_shape=(jax.ShapeDtype...]
where the time goes in v2:
time: 75.6 us; the launch traced here: 75.4 us
  Pallas kernels  70.6 us (93%)
  local copies, waits for them, and re-layouts  4.19 us (6%)
    pallas_call x1, Pallas kernels, shards(): pl.pallas_call(functools.partial(kernel, dims), out_shape=(jax.ShapeDtype...  70.6 us
    unnamed x5, local copies, waits for them, and re-layouts  4.19 us

profile of v2, /device:TPU:0, one launch (start us, length us, event | category | flops | bytes accessed | tf_op | source)
XLA Modules:
  0.0 75.4 jit_solution(11988137998017280665)
XLA Ops:
  0.6 70.6 %shard_map.94 = (f32[256,128]{1,0:T(8,128)}, f32[864,128]{1,0:T(8,128)}, f32[864,128]{1,0:T(8,128)}) custom-call(f32[256,128]{1,0:T(8,128)} %bitcast.13, f32[256,128]{1,0:T(8,128)} %bitcast.14, f32[256,128]{1,0:T(8,128)} %bitcast.15, f32[256,128]{1,0:T(8,128)} %bitcast.16, f32[864,128]{1,0:T(8,128)} %bitcast.9, f32[864,128]{1,0:T(8,128)} %bitcast.10, s32[4]{0:T(128)} %len_ref.1), custom_call_target="tpu_custom_call" | custom-call | tf_op jit(solution)/shard_map/pallas_call | solution.py:400
  71.2 1.6 %copy.13 = f32[2,2,64,128]{3,2,1,0:T(8,128)} copy(f32[2,2,64,128]{3,2,1,0:T(8,128)} %bitcast.17) | data formatting | bytes 262144
  72.8 0.0 copy-start
  72.8 1.9 %copy.14 = f32[27,32,128]{2,1,0:T(8,128)} copy(f32[27,32,128]{2,1,0:T(8,128)} %bitcast.12) | data formatting | bytes 884736
  74.7 0.0 copy-done
  74.7 0.8 %copy.15 = f32[27,32,128]{2,1,0:T(8,128)} copy(f32[27,32,128]{2,1,0:T(8,128)S(1)} %bitcast.11) | data formatting | bytes 884736
Async XLA Ops:
  72.8 1.9 %copy-start = (f32[864,128]{1,0:T(8,128)S(1)}, f32[864,128]{1,0:T(8,128)}, u32[]{:S(2)}) copy-start(f32[864,128]{1,0:T(8,128)} %get-tuple-element.8) | copy-start | bytes 1327108

commit v3 on v2

--- a/solution.py
+++ b/solution.py
@@ -257,16 +257,33 @@
                 sum_hop(g, 1, t, part, rs).start()
 
     def scatter_middle(g, part, rs):
-        for k in range(T - 2):
-            for way, t in ((0, T - 1 - k), (1, k)):
-                inner = (tm > 0) & (tm < t) if way == 0 else (tm < T - 1) & (tm > t)
-
-                @pl.when(inner)
-                def _(way=way, t=t):
-                    c = sum_hop(g, way, t, part, rs)
+        def right():
+            for t in range(T - 1, 1, -1):
+                @pl.when(tm < t)
+                def _(t=t):
+                    c = sum_hop(g, 0, t, part, rs)
                     c.wait_recv()
-                    part[t * B:(t + 1) * B, :] += rs[way, t]
+                    part[t * B:(t + 1) * B, :] += rs[0, t]
                     c.start()
+
+        def left():
+            for t in range(T - 2):
+                @pl.when(tm > t)
+                def _(t=t):
+                    c = sum_hop(g, 1, t, part, rs)
+                    c.wait_recv()
+                    part[t * B:(t + 1) * B, :] += rs[1, t]
+                    c.start()
+
+        @pl.when((tm > 0) & (tm < T // 2))
+        def _():
+            right()
+            left()
+
+        @pl.when((tm < T - 1) & (tm >= T // 2))
+        def _():
+            left()
+            right()
 
     scale = 1.0 / (F * T * H * W) ** 0.5
 
@@ -291,8 +308,8 @@
         def _():
             full_hop(g, 1, tm, full).start()
 
-    def pass_on(g, full):
-        for k in range(1, T):
+    def pass_on(g, full, steps):
+        for k in steps:
             @pl.when(tm - k >= 0)
             def _(k=k):
                 c = full_hop(g, 0, tm - k, full)
@@ -341,7 +358,8 @@
     kernel_grad(gb2, ft2, part2)
     scatter_first(0, part2, rs2)
     weights(w1_ref, wb1)
-    finish(1, chan_buf, near, far, lambda: scatter_middle(0, part2, rs2))
+    finish(1, chan_buf, near, far, lambda: None)
+    scatter_middle(0, part2, rs2)
     for half in range(2):
         for b in range(S):
             for f in range(F):
@@ -355,16 +373,17 @@
     for c in xcopies:
         c.wait_recv()
     turned(lambda b: xr[b], ft1)
+    own_block(0, part2, rs2, full2)
     kernel_grad(gb1, ft1, part1)
     scatter_first(1, part1, rs1)
-    own_block(0, part2, rs2, full2)
+    pass_on(0, full2, range(1, 2))
     result = input_grad(gb1, wb1)
     for b in range(S):
         op[b] = packed_rows(result, b)
     ocopies = exchange(op, orr)
     orr[s] = op[s]
     scatter_middle(1, part1, rs1)
-    pass_on(0, full2)
+    pass_on(0, full2, range(2, T))
     own_block(1, part1, rs1, full1)
     g2_ref[...] = full2[0:27 * CI, :]
     for c in ocopies:
@@ -374,12 +393,18 @@
             j = f * R + r
             gi_ref[j * W:(j + 1) * W, :] = jnp.concatenate(
                 [orr[q, :, j * CI:(j + 1) * CI] for q in range(S)], axis=1)
-    pass_on(1, full1)
+    pass_on(1, full1, range(1, T))
     g1_ref[...] = full1[0:27 * CI, :]
     settle(0, rows_buf, part2, rs2, full2)
     settle(1, chan_buf, part1, rs1, full1)
     for c in sent:
         c.wait_send()
+
+
+def hand_over(a, b, c, x, y, z):
+    x[...] = a[...]
+    y[...] = b[...]
+    z[...] = c[...]
 
 
 def shards(S, T, inputs, pre_first, pre_second, cotangent, weight_first, weight_second, clip_lengths):
@@ -429,6 +454,13 @@
             collective_id=0, has_side_effects=True, vmem_limit_bytes=56 * 1024 * 1024
         ),
     )(flat(inputs), flat(pre_first), flat(pre_second), flat(cotangent), flat(weight_first), flat(weight_second), clip_lengths)
+    anywhere = pl.BlockSpec(memory_space=pltpu.VMEM)
+    gi, g1, g2 = pl.pallas_call(
+        hand_over,
+        out_shape=tuple(jax.ShapeDtypeStruct(v.shape, F32) for v in (gi, g1, g2)),
+        in_specs=[anywhere] * 3,
+        out_specs=(anywhere,) * 3,
+    )(gi, g1, g2)
     return gi.reshape(inputs.shape), g1.reshape(27, CI, C), g2.reshape(27, CI, C)
 
 

time: 75.6 us -> 70.2 us (0.929)
  local copies, waits for them, and re-layouts: 4.19 us -> 0 us
  Pallas kernels: 70.6 us -> 69.4 us
    unnamed x5 -> x0, local copies, waits for them, and re-layouts: 4.19 us -> none
    pallas_call x1, Pallas kernels: 70.6 us -> 67.2 us  [shards(): pl.pallas_call(functools.partial(kernel, dims), out_shape=(jax.ShapeDtype...]
    pallas_call x0 -> x1, Pallas kernels: none -> 2.19 us  [shards(): pl.pallas_call(hand_over, out_shape=tuple((jax.ShapeDtypeStruct(v.shape,...]
where the time goes in v3:
time: 70.2 us; the launch traced here: 70.1 us
  Pallas kernels  69.4 us (99%)
    pallas_call x1, Pallas kernels, shards(): pl.pallas_call(functools.partial(kernel, dims), out_shape=(jax.ShapeDtype...  67.2 us
    pallas_call x1, Pallas kernels, shards(): pl.pallas_call(hand_over, out_shape=tuple((jax.ShapeDtypeStruct(v.shape,...  2.19 us

profile of v3, /device:TPU:0, one launch (start us, length us, event | category | flops | bytes accessed | tf_op | source)
XLA Modules:
  0.0 70.1 jit_solution(10360243578428420410)
XLA Ops:
  0.6 67.2 %shard_map.94 = (f32[256,128]{1,0:T(8,128)}, f32[864,128]{1,0:T(8,128)}, f32[864,128]{1,0:T(8,128)}) custom-call(f32[256,128]{1,0:T(8,128)} %bitcast.11, f32[256,128]{1,0:T(8,128)} %bitcast.12, f32[256,128]{1,0:T(8,128)} %bitcast.13, f32[256,128]{1,0:T(8,128)} %bitcast.14, f32[864,128]{1,0:T(8,128)} %bitcast.9, f32[864,128]{1,0:T(8,128)} %bitcast.10, s32[4]{0:T(128)} %len_ref.1), custom_call_target="tpu_custom_call" | custom-call | tf_op jit(solution)/shard_map/pallas_call | solution.py:425
  67.9 2.2 %shard_map.95 = (f32[256,128]{1,0:T(8,128)}, f32[864,128]{1,0:T(8,128)}, f32[864,128]{1,0:T(8,128)}) custom-call(f32[256,128]{1,0:T(8,128)} %get-tuple-element.9.a, f32[864,128]{1,0:T(8,128)} %get-tuple-element.10.b, f32[864,128]{1,0:T(8,128)} %get-tuple-element.11.c), custom_call_target="tpu_custom_call" | custom-call | tf_op jit(solution)/shard_map/pallas_call | solution.py:458
